TPU v7x, 32 devices: a whole 2x2x4 slice. The times are simulated.
32 devices in a mesh: blk: 8 (over z, x), ulysses: 4 (over y, core).
Axes of the slice: x: 2, y: 2, z: 4, core: 2. Of those that a mesh axis runs over, the one named last changes fastest.
Arguments:
- tokens: bfloat16 [2, 2048, 768], P(None, ('blk', 'ulysses')), may hold values from -6 to 6
- attn_gain: bfloat16 [768], P(('blk', 'ulysses')), may hold values from 0.25 to 1.75
- qkv_weight: bfloat16 [768, 2304], P(('blk', 'ulysses')), may hold values from -0.3125 to 0.3125
- attn_out_weight: bfloat16 [768, 768], P(('blk', 'ulysses')), may hold values from -1.25 to 1.25
- mlp_gain: bfloat16 [768], P(('blk', 'ulysses')), may hold values from 0.25 to 1.75
- in_weight: bfloat16 [768, 2304], P(('blk', 'ulysses')), may hold values from -0.21875 to 0.21875
- out_weight: bfloat16 [1152, 768], P(None, ('blk', 'ulysses')), may hold values from -0.1875 to 0.1875
- cotangent: bfloat16 [2, 2048, 768], P(None, ('blk', 'ulysses')), may hold values from -6 to 6
Outputs:
- layer_output: bfloat16 [2, 2048, 768], P(None, ('blk', 'ulysses'))
- input_grad: bfloat16 [2, 2048, 768], P(None, ('blk', 'ulysses'))
- attn_gain_grad: float32 [768], P(('blk', 'ulysses'))
- qkv_weight_grad: float32 [768, 2304], P(('blk', 'ulysses'))
- attn_out_weight_grad: float32 [768, 768], P(('blk', 'ulysses'))
- mlp_gain_grad: float32 [768], P(('blk', 'ulysses'))
- in_weight_grad: float32 [768, 2304], P(('blk', 'ulysses'))
- out_weight_grad: float32 [1152, 768], P(None, ('blk', 'ulysses'))
All inputs are finite; a program needn't handle non-finite values.
Results may differ from a plain program's by a relative error of at most 0.018.
The roundings to bfloat16 on the way count: a program that leaves them out, or rounds other values in their place, can miss the bound.
Values may be sent and summed in bfloat16 or wider, within the bound.
No kernel may reach another device: no remote copies, remote signals or barrier semaphores. Data moves between devices by JAX's collectives and lax.ppermute only.
A program may use at most 256 MiB of HBM per device.

v0:
```python
import jax
import jax.numpy as jnp
from jax import lax
from jax.sharding import PartitionSpec as P

HEAD = 64
EPSILON = 1e-05
THETA = 160000.0


def from_behind(value, axis, by):
    size = lax.axis_size(axis)
    return lax.ppermute(value, axis, [(i, (i + by) % size) for i in range(size)])


def normalize(values):
    center = values - jnp.mean(values, axis=-1, keepdims=True)
    inverse = lax.rsqrt(jnp.mean(center * center, axis=-1, keepdims=True) + EPSILON)
    return (center * inverse, inverse)


def norm_back(grad_normed, normed, inverse):
    first_mean = jnp.mean(grad_normed, axis=-1, keepdims=True)
    second_mean = jnp.mean(grad_normed * normed, axis=-1, keepdims=True)
    return inverse * (grad_normed - first_mean - normed * second_mean)


def rotation(first_row, row_count, head_width):
    half_width = head_width // 2
    frequency = THETA ** (-(jnp.arange(half_width, dtype=jnp.float32) * 2.0) / head_width)
    positions = (first_row + jnp.arange(row_count, dtype=jnp.int32)).astype(jnp.float32)
    angles = positions[:, None] * frequency[None, :]
    cosine_table = jnp.concatenate([jnp.cos(angles), jnp.cos(angles)], axis=-1)
    sine_table = jnp.concatenate([jnp.sin(angles), jnp.sin(angles)], axis=-1)
    return (cosine_table, sine_table)


def rotate(values, cosine_table, sine_table, direction):
    half_width = values.shape[-1] // 2
    turned = jnp.concatenate([-values[..., half_width:], values[..., :half_width]], axis=-1)
    return values * cosine_table[:, None, :] + direction * turned * sine_table[:, None, :]


def block_grads(
    query_part,
    key_part,
    value_part,
    grad_part,
    log_part,
    dots_part,
    top_part,
    total_part,
    score_scale,
):
    scores = (
        jnp.einsum("sqhd,skhd->shqk", query_part, key_part, preferred_element_type=jnp.float32)
        * score_scale
    )
    probs = jnp.exp(scores - log_part[..., None])
    grad_probs = jnp.einsum(
        "sqhd,skhd->shqk", grad_part, value_part, preferred_element_type=jnp.float32
    )
    grad_scores = (probs * (grad_probs - dots_part[..., None])).astype(jnp.bfloat16)
    weights_low = jnp.exp(scores - top_part[..., None]).astype(jnp.bfloat16)
    grad_scaled = grad_part.astype(jnp.float32) / jnp.transpose(total_part, (0, 2, 1))[..., None]
    value_term = jnp.einsum("shqk,sqhd->skhd", weights_low.astype(jnp.float32), grad_scaled)
    return (value_term, grad_scores)


def body(
    tokens, attn_gain, qkv_weight, attn_out_weight, mlp_gain, in_weight, out_weight, cotangent
):
    sequences, per_device, model_width = tokens.shape
    groups = lax.axis_size("ulysses")
    cycle_size = lax.axis_size("blk")
    group_width = model_width // groups
    heads_here = group_width // HEAD
    group_rows = per_device * groups
    score_scale = HEAD ** (-0.5)
    qkv_full, attn_full, in_full, out_full, gain_one, gain_two = (
        lax.all_gather(qkv_weight, ("blk", "ulysses"), axis=0, tiled=True),
        lax.all_gather(attn_out_weight, ("blk", "ulysses"), axis=0, tiled=True),
        lax.all_gather(in_weight, ("blk", "ulysses"), axis=0, tiled=True),
        lax.all_gather(out_weight, ("blk", "ulysses"), axis=1, tiled=True),
        lax.all_gather(attn_gain, ("blk", "ulysses"), axis=0, tiled=True),
        lax.all_gather(mlp_gain, ("blk", "ulysses"), axis=0, tiled=True),
    )
    gain_one = gain_one.astype(jnp.float32)
    gain_two = gain_two.astype(jnp.float32)
    hidden_units = out_full.shape[0]
    inputs_wide = tokens.astype(jnp.float32).reshape(sequences * per_device, model_width)
    normed_one, inverse_one = normalize(inputs_wide)
    hidden_one = (normed_one * gain_one).astype(jnp.bfloat16)
    qkv = jnp.dot(hidden_one, qkv_full, preferred_element_type=jnp.float32).astype(jnp.bfloat16)
    packed = qkv.reshape(sequences, per_device, 3, groups, group_width)
    headwise = lax.all_to_all(packed, "ulysses", split_axis=3, concat_axis=1, tiled=True)
    headwise = headwise.reshape(sequences, group_rows, 3, heads_here, HEAD)
    cosine_table, sine_table = rotation(lax.axis_index("blk") * group_rows, group_rows, HEAD)
    queries = rotate(headwise[:, :, 0].astype(jnp.float32), cosine_table, sine_table, 1.0).astype(
        jnp.bfloat16
    )
    key_rows = rotate(headwise[:, :, 1].astype(jnp.float32), cosine_table, sine_table, 1.0).astype(
        jnp.bfloat16
    )
    value_rows = headwise[:, :, 2]
    start_top = jnp.full((sequences, heads_here, group_rows), -1e30, jnp.float32)
    zeros_rows = jnp.zeros((sequences, group_rows, heads_here, HEAD), jnp.float32)
    key_piece = lax.all_gather(key_rows, "blk", axis=1, tiled=True)
    value_piece = lax.all_gather(value_rows, "blk", axis=1, tiled=True)
    scores = (
        jnp.einsum("sqhd,skhd->shqk", queries, key_piece, preferred_element_type=jnp.float32)
        * score_scale
    )
    new_top = jnp.maximum(start_top, jnp.max(scores, axis=-1))
    weights = jnp.exp(scores - new_top[..., None])
    attend_row_total = jnp.sum(weights, axis=-1)
    update = jnp.einsum(
        "shqk,skhd->sqhd",
        weights.astype(jnp.bfloat16),
        value_piece,
        preferred_element_type=jnp.float32,
    )
    weighted = update
    row_top, row_total, weighted = (new_top, attend_row_total, weighted)
    log_total = row_top + jnp.log(row_total)
    attn_wide = weighted / jnp.transpose(row_total, (0, 2, 1))[..., None]
    attn_low = attn_wide.astype(jnp.bfloat16).reshape(sequences, group_rows, 1, group_width)
    token_rows = lax.all_to_all(attn_low, "ulysses", split_axis=1, concat_axis=2, tiled=True)
    attn_cat = token_rows.reshape(sequences * per_device, model_width)
    middle = inputs_wide + jnp.dot(attn_cat, attn_full, preferred_element_type=jnp.float32)
    normed_two, inverse_two = normalize(middle)
    hidden_two = (normed_two * gain_two).astype(jnp.bfloat16)
    joint = jnp.dot(hidden_two, in_full, preferred_element_type=jnp.float32)

    def geglu(joint_pre):
        return (
            jax.nn.gelu(joint_pre[:, :hidden_units], approximate=False)
            * joint_pre[:, hidden_units:]
        )

    act_wide, geglu_back = jax.vjp(geglu, joint)
    activation = act_wide.astype(jnp.bfloat16)
    result = middle + jnp.dot(activation, out_full, preferred_element_type=jnp.float32)
    layer_output = result.astype(jnp.bfloat16).reshape(sequences, per_device, model_width)
    grad_out = cotangent.reshape(sequences * per_device, model_width)
    grad_wout = jnp.einsum("tf,td->fd", activation, grad_out, preferred_element_type=jnp.float32)
    grad_act = jnp.einsum("td,fd->tf", grad_out, out_full, preferred_element_type=jnp.float32)
    grad_joint = geglu_back(grad_act)[0].astype(jnp.bfloat16)
    grad_win = jnp.einsum("tc,tf->cf", hidden_two, grad_joint, preferred_element_type=jnp.float32)
    grad_hidden_two = jnp.einsum(
        "tf,cf->tc", grad_joint, in_full, preferred_element_type=jnp.float32
    )
    grad_gain_two = jnp.sum(grad_hidden_two * normed_two, axis=0)
    grad_middle = grad_out.astype(jnp.float32) + norm_back(
        grad_hidden_two * gain_two, normed_two, inverse_two
    )
    grad_branch = grad_middle.astype(jnp.bfloat16)
    grad_wattn = jnp.einsum("tc,td->cd", attn_cat, grad_branch, preferred_element_type=jnp.float32)
    grad_cat = jnp.einsum(
        "td,cd->tc", grad_branch, attn_full, preferred_element_type=jnp.float32
    ).astype(jnp.bfloat16)
    grad_heads_in = lax.all_to_all(
        grad_cat.reshape(sequences, per_device, groups, group_width),
        "ulysses",
        split_axis=2,
        concat_axis=1,
        tiled=True,
    )
    grad_attn = grad_heads_in.reshape(sequences, group_rows, heads_here, HEAD)
    row_dots = jnp.transpose(jnp.sum(grad_attn.astype(jnp.float32) * attn_wide, axis=-1), (0, 2, 1))

    def cycle_step(step_index, state_now):
        key_now, value_now, grad_key, grad_value, grad_query = state_now
        value_term, grad_scores = block_grads(
            queries,
            key_now,
            value_now,
            grad_attn,
            log_total,
            row_dots,
            row_top,
            row_total,
            score_scale,
        )
        grad_value = grad_value + value_term
        grad_key = grad_key + score_scale * jnp.einsum(
            "shqk,sqhd->skhd", grad_scores, queries, preferred_element_type=jnp.float32
        )
        grad_query = grad_query + score_scale * jnp.einsum(
            "shqk,skhd->sqhd", grad_scores, key_now, preferred_element_type=jnp.float32
        )
        key_now, value_now = from_behind((key_now, value_now), "blk", 1)
        grad_key, grad_value = (
            from_behind(grad_key.astype(jnp.bfloat16), "blk", 1).astype(grad_key.dtype),
            from_behind(grad_value.astype(jnp.bfloat16), "blk", 1).astype(grad_value.dtype),
        )
        return (key_now, value_now, grad_key, grad_value, grad_query)

    final_state = lax.fori_loop(
        0, cycle_size, cycle_step, (key_rows, value_rows, zeros_rows, zeros_rows, zeros_rows)
    )
    grad_key, grad_value, grad_query = (final_state[2], final_state[3], final_state[4])
    grad_query = rotate(grad_query, cosine_table, sine_table, -1.0)
    grad_key = rotate(grad_key, cosine_table, sine_table, -1.0)
    grad_stack = jnp.stack([grad_query, grad_key, grad_value], axis=2).astype(jnp.bfloat16)
    grad_stack = grad_stack.reshape(sequences, group_rows, 3, 1, group_width)
    grad_tokens = lax.all_to_all(grad_stack, "ulysses", split_axis=1, concat_axis=3, tiled=True)
    grad_qkv = grad_tokens.reshape(sequences * per_device, 3 * model_width)
    grad_wqkv = jnp.einsum("tc,tf->cf", hidden_one, grad_qkv, preferred_element_type=jnp.float32)
    grad_hidden_one = jnp.einsum(
        "tf,cf->tc", grad_qkv, qkv_full, preferred_element_type=jnp.float32
    )
    grad_gain_one = jnp.sum(grad_hidden_one * normed_one, axis=0)
    grad_input = grad_middle + norm_back(grad_hidden_one * gain_one, normed_one, inverse_one)
    input_grad = grad_input.astype(jnp.bfloat16).reshape(sequences, per_device, model_width)
    shard_qkv, shard_attn, shard_in, shard_out, shard_one, shard_two = (
        lax.psum_scatter(grad_wqkv, ("blk", "ulysses"), scatter_dimension=0, tiled=True),
        lax.psum_scatter(grad_wattn, ("blk", "ulysses"), scatter_dimension=0, tiled=True),
        lax.psum_scatter(grad_win, ("blk", "ulysses"), scatter_dimension=0, tiled=True),
        lax.psum_scatter(grad_wout, ("blk", "ulysses"), scatter_dimension=1, tiled=True),
        lax.psum_scatter(grad_gain_one, ("blk", "ulysses"), scatter_dimension=0, tiled=True),
        lax.psum_scatter(grad_gain_two, ("blk", "ulysses"), scatter_dimension=0, tiled=True),
    )
    return (
        layer_output,
        input_grad,
        shard_one,
        shard_qkv,
        shard_attn,
        shard_two,
        shard_in,
        shard_out,
    )


def solution(mesh):
    placed = (
        P(None, ("blk", "ulysses"), None),
        P(("blk", "ulysses")),
        P(("blk", "ulysses"), None),
        P(("blk", "ulysses"), None),
        P(("blk", "ulysses")),
        P(("blk", "ulysses"), None),
        P(None, ("blk", "ulysses")),
        P(None, ("blk", "ulysses"), None),
    )
    return jax.shard_map(
        body,
        mesh=mesh,
        in_specs=placed,
        out_specs=(
            P(None, ("blk", "ulysses"), None),
            P(None, ("blk", "ulysses"), None),
            P(("blk", "ulysses")),
            P(("blk", "ulysses"), None),
            P(("blk", "ulysses"), None),
            P(("blk", "ulysses")),
            P(("blk", "ulysses"), None),
            P(None, ("blk", "ulysses")),
        ),
        check_vma=False,
    )
```

profile of v0, /device:TPU:0, one launch (start us, length us, event | category | flops | bytes accessed | tf_op | source)
XLA Modules:
  0.0 867.9 jit_solution(4147596167485549714)
XLA Ops:
  9.6 42.2 %all-reduce.8 = (bf16[768]{0:T(1024)(128)(2,1)S(1)}, bf16[768]{0:T(1024)(128)(2,1)S(1)}) all-reduce(bf16[768]{0:T(1024)(128)(2,1)S(1)} %dynamic-update-slice, bf16[768]{0:T(1024)(128)(2,1)S(1)} %dynamic-update-slice.1), channel_id=1, replica_groups=mesh['blk'=8,'ulysses'=4] {'blk','ulysses'}, use_global_device_ids=true, to_apply=%add.2 | all-reduce | flops 1536 | bytes 6144
  55.8 18.1 %all-gather.8.cloned.1.call-done = bf16[768,2304]{1,0:T(8,128)(2,1)} async-done(((bf16[24,2304]{1,0:T(8,128)(2,1)}), bf16[768,2304]{1,0:T(8,128)(2,1)}) %all-gather.8.cloned.1.call-update) | async-done | bytes 3538960 | tf_op jit(solution)/shard_map/all_gather | solution.py:81
  82.7 10.7 %all-to-all-done = bf16[2,64,3,4,192]{4,1,2,0,3:T(8,128)(2,1)S(1)} async-done(((bf16[2,64,3,4,192]{4,1,2,0,3:T(8,128)(2,1)}), bf16[2,64,3,4,192]{4,1,2,0,3:T(8,128)(2,1)S(1)}, u32[]{:S(2)}, u32[]{:S(2)}) %all-to-all-start) | async-done | bytes 589856 | tf_op jit(solution)/shard_map/all_to_all | solution.py:96
  99.1 41.7 %all-gather.10.cloned.1.call-done = bf16[2,2048,3,64]{1,3,2,0:T(8,128)(2,1)} async-done(((bf16[2,256,3,64]{1,3,2,0:T(8,128)(2,1)}), bf16[2,2048,3,64]{1,3,2,0:T(8,128)(2,1)}) %all-gather.10.cloned.1.call-update) | async-done | bytes 1572880 | tf_op jit(solution)/shard_map/all_gather | solution.py:108
  144.2 4.5 copy-done
  151.1 35.8 %all-gather.18.cloned.1.call-done = bf16[2,2048,1,3,64]{1,4,3,0,2:T(8,128)(2,1)} async-done(((bf16[2,256,1,3,64]{1,4,3,0,2:T(8,128)(2,1)}), bf16[2,2048,1,3,64]{1,4,3,0,2:T(8,128)(2,1)}) %all-gather.18.cloned.1.call-update) | async-done | bytes 1572880 | tf_op jit(solution)/shard_map/all_gather | solution.py:109
  186.9 8.2 fusion.56
  199.6 5.8 all-to-all-done.1
  205.9 36.1 %all-gather.12.cloned.1.call-done = bf16[768,768]{1,0:T(8,128)(2,1)} async-done(((bf16[24,768]{1,0:T(8,128)(2,1)}), bf16[768,768]{1,0:T(8,128)(2,1)}) %all-gather.12.cloned.1.call-update) | async-done | bytes 1179664 | tf_op jit(solution)/shard_map/all_gather | solution.py:82
  244.0 59.9 %all-gather.14.cloned.1.call-done = bf16[768,2304]{1,0:T(8,128)(2,1)} async-done(((bf16[24,2304]{1,0:T(8,128)(2,1)}), bf16[768,2304]{1,0:T(8,128)(2,1)}) %all-gather.14.cloned.1.call-update) | async-done | bytes 3538960 | tf_op jit(solution)/shard_map/all_gather | solution.py:83
  306.6 54.5 %all-gather.16.cloned.1.call-done = bf16[1152,768]{0,1:T(8,128)(2,1)} async-done(((bf16[1152,24]{0,1:T(8,128)(2,1)}), bf16[1152,768]{0,1:T(8,128)(2,1)}) %all-gather.16.cloned.1.call-update) | async-done | bytes 1769488 | tf_op jit(solution)/shard_map/all_gather | solution.py:84
  379.2 4.7 fusion.49
  387.3 184.9 %while.19 = (s32[]{:T(128)}, bf16[2,256,3,64]{1,3,2,0:T(8,128)(2,1)}, bf16[2,256,3,64]{1,3,2,0:T(8,128)(2,1)}, f32[2,256,3,64]{1,3,2,0:T(8,128)}, f32[2,256,3,64...) while((s32[]{:T(128)}, ...), condition=%wide.region_10.0_spmd.clone, body=%wide.region_9.0_spmd.clone.sunk | while | flops 255787008 | bytes 18751904 | solution.py:199
  399.7 7.6 collective-permute-done.2
  422.4 14.6 %collective-permute-done.2 = bf16[2,256,3,64]{1,3,2,0:T(8,128)(2,1)} collective-permute-done((bf16[2,256,3,64]{1,3,2,0:T(8,128)(2,1)}, bf16[2,256,3,64]{1,3,2,0:T(8,128)(2,1)}, u32[]{:S(2)}, u32[]{:S(2)}) %collective-permute-start.2) | collective-permute-done | bytes 196640 | tf_op jit(solution)/shard_map/while/body/eval_jaxpr/ppermute | solution.py:13
  449.1 12.9 %collective-permute-done.2 = bf16[2,256,3,64]{1,3,2,0:T(8,128)(2,1)} collective-permute-done((bf16[2,256,3,64]{1,3,2,0:T(8,128)(2,1)}, bf16[2,256,3,64]{1,3,2,0:T(8,128)(2,1)}, u32[]{:S(2)}, u32[]{:S(2)}) %collective-permute-start.2) | collective-permute-done | bytes 196640 | tf_op jit(solution)/shard_map/while/body/eval_jaxpr/ppermute | solution.py:13
  474.0 10.6 %collective-permute-done.2 = bf16[2,256,3,64]{1,3,2,0:T(8,128)(2,1)} collective-permute-done((bf16[2,256,3,64]{1,3,2,0:T(8,128)(2,1)}, bf16[2,256,3,64]{1,3,2,0:T(8,128)(2,1)}, u32[]{:S(2)}, u32[]{:S(2)}) %collective-permute-start.2) | collective-permute-done | bytes 196640 | tf_op jit(solution)/shard_map/while/body/eval_jaxpr/ppermute | solution.py:13
  496.6 8.0 collective-permute-done.2
  558.5 11.0 %collective-permute-done.2 = bf16[2,256,3,64]{1,3,2,0:T(8,128)(2,1)} collective-permute-done((bf16[2,256,3,64]{1,3,2,0:T(8,128)(2,1)}, bf16[2,256,3,64]{1,3,2,0:T(8,128)(2,1)}, u32[]{:S(2)}, u32[]{:S(2)}) %collective-permute-start.2) | collective-permute-done | bytes 196640 | tf_op jit(solution)/shard_map/while/body/eval_jaxpr/ppermute | solution.py:13
  577.6 5.3 all-to-all-start.3
  583.1 11.5 %all-to-all-done.3 = bf16[2,256,3,1,192]{4,0,3,2,1:T(2,128)(2,1)S(1)} async-done(((bf16[2,256,3,1,192]{4,0,3,2,1:T(2,128)(2,1)}), bf16[2,256,3,1,192]{4,0,3,2,1:T(2,128)(2,1)S(1)}, u32[]{:S(2)}, u32[]{:S(2)}) %all-to-all-start.3) | async-done | bytes 589856 | tf_op jit(solution)/shard_map/all_to_all | solution.py:207
  606.4 37.0 %all-reduce.7 = (f32[768]{0:T(1024)S(1)}, f32[768]{0:T(1024)S(1)}) all-reduce(f32[768]{0:T(1024)S(1)} %get-tuple-element.116, f32[768]{0:T(1024)S(1)} %copy-done.28), channel_id=3, replica_groups=mesh['blk'=8,'ulysses'=4] {'blk','ulysses'}, use_global_device_ids=true, to_apply=%region_14.0.clone | all-reduce | flops 1536 | bytes 12288
  645.5 91.0 %reduce-scatter.11.cloned.1.call-done = f32[24,2304]{1,0:T(8,128)} async-done(((f32[768,2304]{1,0:T(8,128)}), f32[24,2304]{1,0:T(8,128)}) %reduce-scatter.11.cloned.1.call-update) | async-done | bytes 221200 | tf_op jit(solution)/shard_map/reduce_scatter | solution.py:219
  736.5 124.6 %reduce-scatter.7.cloned.1.call-done = f32[24,2304]{1,0:T(8,128)} async-done(((f32[768,2304]{1,0:T(8,128)}), f32[24,2304]{1,0:T(8,128)}) %reduce-scatter.7.cloned.1.call-update) | async-done | bytes 221200 | tf_op jit(solution)/shard_map/reduce_scatter | solution.py:217
  (361 shorter events, 196.3 us)
Async XLA Ops:
  7.2 66.7 %all-gather.8.cloned.1.call-start = ((), (), s32[]{:S(2)}) async-start(), calls=%async_computation.8 | async-start | bytes 3649536 | tf_op jit(solution)/shard_map/all_gather | solution.py:81
  81.8 59.0 %all-gather.10.cloned.1.call-start = ((), (), s32[]{:S(2)}) async-start(), calls=%async_computation.9 | async-start | bytes 1769472 | tf_op jit(solution)/shard_map/all_gather | solution.py:108
  96.6 90.3 %all-gather.18.cloned.1.call-start = ((), (), s32[]{:S(2)}) async-start(), calls=%async_computation.16 | async-start | bytes 1769472 | tf_op jit(solution)/shard_map/all_gather | solution.py:109
  97.3 144.7 %all-gather.12.cloned.1.call-start = ((), (), s32[]{:S(2)}) async-start(), calls=%async_computation.10 | async-start | bytes 1216512 | tf_op jit(solution)/shard_map/all_gather | solution.py:82
  97.9 206.0 %all-gather.14.cloned.1.call-start = ((), (), s32[]{:S(2)}) async-start(), calls=%async_computation.11 | async-start | bytes 3649536 | tf_op jit(solution)/shard_map/all_gather | solution.py:83
  98.5 262.6 %all-gather.16.cloned.1.call-start = ((), (), s32[]{:S(2)}) async-start(), calls=%async_computation.12 | async-start | bytes 1824768 | tf_op jit(solution)/shard_map/all_gather | solution.py:84
  199.4 446.1 %reduce-scatter.9.cloned.1.call-start = ((), (), s32[]{:S(2)}) async-start(), calls=%async_computation.14 | async-start | bytes 2433024 | tf_op jit(solution)/shard_map/reduce_scatter | solution.py:218
  368.7 276.7 %reduce-scatter.13.cloned.1.call-start = ((), (), s32[]{:S(2)}) async-start(), calls=%async_computation.17 | async-start | bytes 3649536
  379.1 357.4 %reduce-scatter.11.cloned.1.call-start = ((), (), s32[]{:S(2)}) async-start(), calls=%async_computation.15 | async-start | bytes 7299072 | tf_op jit(solution)/shard_map/reduce_scatter | solution.py:219
  388.3 22.6 %collective-permute-start = (bf16[2,256,3,64]{1,3,2,0:T(8,128)(2,1)S(1)}, bf16[2,256,3,64]{1,3,2,0:T(8,128)(2,1)}, u32[]{:S(2)}, u32[]{:S(2)}) collective-permute-start(bf16[2,256,3,64]{1,3,2,0:T(8,128)(2,1)S(1)} %copy.62), channel_id=1, source_target_pairs={{0,4},{4,8},{8,12},{12,16},{16,20},{20,24},{24,28},{28,0},{1,5},{5... | collective-permute-start | bytes 589832 | tf_op jit(solution)/shard_map/while/body/eval_jaxpr/ppermute | solution.py:13
  390.6 20.3 %collective-permute-start.1 = (bf16[2,256,3,64]{1,3,2,0:T(8,128)(2,1)S(1)}, bf16[2,256,3,64]{1,3,2,0:T(8,128)(2,1)}, u32[]{:S(2)}, u32[]{:S(2)}) collective-permute-start(bf16[2,256,3,64]{1,3,2,0:T(8,128)(2,1)S(1)} %copy.63), channel_id=1, source_target_pairs={{0,4},{4,8},{8,12},{12,16},{16,20},{20,24},{24,28},{28,0},{1,5},{5... | collective-permute-start | bytes 589832 | tf_op jit(solution)/shard_map/while/body/eval_jaxpr/ppermute | solution.py:13
  411.8 28.1 %collective-permute-start = (bf16[2,256,3,64]{1,3,2,0:T(8,128)(2,1)S(1)}, bf16[2,256,3,64]{1,3,2,0:T(8,128)(2,1)}, u32[]{:S(2)}, u32[]{:S(2)}) collective-permute-start(bf16[2,256,3,64]{1,3,2,0:T(8,128)(2,1)S(1)} %copy.62), channel_id=1, source_target_pairs={{0,4},{4,8},{8,12},{12,16},{16,20},{20,24},{24,28},{28,0},{1,5},{5... | collective-permute-start | bytes 589832 | tf_op jit(solution)/shard_map/while/body/eval_jaxpr/ppermute | solution.py:13
  412.7 27.1 %collective-permute-start.1 = (bf16[2,256,3,64]{1,3,2,0:T(8,128)(2,1)S(1)}, bf16[2,256,3,64]{1,3,2,0:T(8,128)(2,1)}, u32[]{:S(2)}, u32[]{:S(2)}) collective-permute-start(bf16[2,256,3,64]{1,3,2,0:T(8,128)(2,1)S(1)} %copy.63), channel_id=1, source_target_pairs={{0,4},{4,8},{8,12},{12,16},{16,20},{20,24},{24,28},{28,0},{1,5},{5... | collective-permute-start | bytes 589832 | tf_op jit(solution)/shard_map/while/body/eval_jaxpr/ppermute | solution.py:13
  415.9 21.1 %collective-permute-start.2 = (bf16[2,256,3,64]{1,3,2,0:T(8,128)(2,1)}, bf16[2,256,3,64]{1,3,2,0:T(8,128)(2,1)}, u32[]{:S(2)}, u32[]{:S(2)}) collective-permute-start(bf16[2,256,3,64]{1,3,2,0:T(8,128)(2,1)} %fusion.109), channel_id=1, source_target_pairs={{0,4},{4,8},{8,12},{12,16},{16,20},{20,24},{24,28},{28,0},{1,5},{5... | collective-permute-start | bytes 589832 | tf_op jit(solution)/shard_map/while/body/eval_jaxpr/ppermute | solution.py:13
  418.5 20.6 %collective-permute-start.3 = (bf16[2,256,3,64]{1,3,2,0:T(8,128)(2,1)}, bf16[2,256,3,64]{1,3,2,0:T(8,128)(2,1)S(1)}, u32[]{:S(2)}, u32[]{:S(2)}) collective-permute-start(bf16[2,256,3,64]{1,3,2,0:T(8,128)(2,1)} %fusion.110), channel_id=1, source_target_pairs={{0,4},{4,8},{8,12},{12,16},{16,20},{20,24},{24,28},{28,0},{1,5},{5... | collective-permute-start | bytes 589832 | tf_op jit(solution)/shard_map/while/body/eval_jaxpr/ppermute | solution.py:13
  440.8 24.1 %collective-permute-start = (bf16[2,256,3,64]{1,3,2,0:T(8,128)(2,1)S(1)}, bf16[2,256,3,64]{1,3,2,0:T(8,128)(2,1)}, u32[]{:S(2)}, u32[]{:S(2)}) collective-permute-start(bf16[2,256,3,64]{1,3,2,0:T(8,128)(2,1)S(1)} %copy.62), channel_id=1, source_target_pairs={{0,4},{4,8},{8,12},{12,16},{16,20},{20,24},{24,28},{28,0},{1,5},{5... | collective-permute-start | bytes 589832 | tf_op jit(solution)/shard_map/while/body/eval_jaxpr/ppermute | solution.py:13
  441.7 23.2 %collective-permute-start.1 = (bf16[2,256,3,64]{1,3,2,0:T(8,128)(2,1)S(1)}, bf16[2,256,3,64]{1,3,2,0:T(8,128)(2,1)}, u32[]{:S(2)}, u32[]{:S(2)}) collective-permute-start(bf16[2,256,3,64]{1,3,2,0:T(8,128)(2,1)S(1)} %copy.63), channel_id=1, source_target_pairs={{0,4},{4,8},{8,12},{12,16},{16,20},{20,24},{24,28},{28,0},{1,5},{5... | collective-permute-start | bytes 589832 | tf_op jit(solution)/shard_map/while/body/eval_jaxpr/ppermute | solution.py:13
  465.8 21.6 %collective-permute-start = (bf16[2,256,3,64]{1,3,2,0:T(8,128)(2,1)S(1)}, bf16[2,256,3,64]{1,3,2,0:T(8,128)(2,1)}, u32[]{:S(2)}, u32[]{:S(2)}) collective-permute-start(bf16[2,256,3,64]{1,3,2,0:T(8,128)(2,1)S(1)} %copy.62), channel_id=1, source_target_pairs={{0,4},{4,8},{8,12},{12,16},{16,20},{20,24},{24,28},{28,0},{1,5},{5... | collective-permute-start | bytes 589832 | tf_op jit(solution)/shard_map/while/body/eval_jaxpr/ppermute | solution.py:13
  466.7 20.7 %collective-permute-start.1 = (bf16[2,256,3,64]{1,3,2,0:T(8,128)(2,1)S(1)}, bf16[2,256,3,64]{1,3,2,0:T(8,128)(2,1)}, u32[]{:S(2)}, u32[]{:S(2)}) collective-permute-start(bf16[2,256,3,64]{1,3,2,0:T(8,128)(2,1)S(1)} %copy.63), channel_id=1, source_target_pairs={{0,4},{4,8},{8,12},{12,16},{16,20},{20,24},{24,28},{28,0},{1,5},{5... | collective-permute-start | bytes 589832 | tf_op jit(solution)/shard_map/while/body/eval_jaxpr/ppermute | solution.py:13
  488.4 19.0 %collective-permute-start = (bf16[2,256,3,64]{1,3,2,0:T(8,128)(2,1)S(1)}, bf16[2,256,3,64]{1,3,2,0:T(8,128)(2,1)}, u32[]{:S(2)}, u32[]{:S(2)}) collective-permute-start(bf16[2,256,3,64]{1,3,2,0:T(8,128)(2,1)S(1)} %copy.62), channel_id=1, source_target_pairs={{0,4},{4,8},{8,12},{12,16},{16,20},{20,24},{24,28},{28,0},{1,5},{5... | collective-permute-start | bytes 589832 | tf_op jit(solution)/shard_map/while/body/eval_jaxpr/ppermute | solution.py:13
  527.6 18.5 %collective-permute-start = (bf16[2,256,3,64]{1,3,2,0:T(8,128)(2,1)S(1)}, bf16[2,256,3,64]{1,3,2,0:T(8,128)(2,1)}, u32[]{:S(2)}, u32[]{:S(2)}) collective-permute-start(bf16[2,256,3,64]{1,3,2,0:T(8,128)(2,1)S(1)} %copy.62), channel_id=1, source_target_pairs={{0,4},{4,8},{8,12},{12,16},{16,20},{20,24},{24,28},{28,0},{1,5},{5... | collective-permute-start | bytes 589832 | tf_op jit(solution)/shard_map/while/body/eval_jaxpr/ppermute | solution.py:13
  547.0 25.2 %collective-permute-start = (bf16[2,256,3,64]{1,3,2,0:T(8,128)(2,1)S(1)}, bf16[2,256,3,64]{1,3,2,0:T(8,128)(2,1)}, u32[]{:S(2)}, u32[]{:S(2)}) collective-permute-start(bf16[2,256,3,64]{1,3,2,0:T(8,128)(2,1)S(1)} %copy.62), channel_id=1, source_target_pairs={{0,4},{4,8},{8,12},{12,16},{16,20},{20,24},{24,28},{28,0},{1,5},{5... | collective-permute-start | bytes 589832 | tf_op jit(solution)/shard_map/while/body/eval_jaxpr/ppermute | solution.py:13
  547.9 24.3 %collective-permute-start.1 = (bf16[2,256,3,64]{1,3,2,0:T(8,128)(2,1)S(1)}, bf16[2,256,3,64]{1,3,2,0:T(8,128)(2,1)}, u32[]{:S(2)}, u32[]{:S(2)}) collective-permute-start(bf16[2,256,3,64]{1,3,2,0:T(8,128)(2,1)S(1)} %copy.63), channel_id=1, source_target_pairs={{0,4},{4,8},{8,12},{12,16},{16,20},{20,24},{24,28},{28,0},{1,5},{5... | collective-permute-start | bytes 589832 | tf_op jit(solution)/shard_map/while/body/eval_jaxpr/ppermute | solution.py:13
  582.9 278.1 %reduce-scatter.7.cloned.1.call-start = ((), (), s32[]{:S(2)}) async-start(), calls=%async_computation.13 | async-start | bytes 7299072 | tf_op jit(solution)/shard_map/reduce_scatter | solution.py:217
  (88 other events, 975.1 us)
Sparse Core Ops, SparseCore 0:
  10.9 62.8 all-gather.7
  96.7 44.0 all-gather.9
  143.4 43.4 all-gather.17
  189.7 52.2 all-gather.11
  244.8 59.0 all-gather.13
  306.6 54.4 all-gather.15
  368.8 114.1 reduce-scatter.8
  489.9 121.3 reduce-scatter.12
  618.6 117.8 reduce-scatter.10
  742.6 118.4 reduce-scatter.6
where the time goes:
time: 870 us; the launch traced here: 868 us
  waiting for transfers between devices  570 us (66%)
  matrix products  99.2 us (11%)
  blocking collectives  79.2 us (9%)
  local copies, waits for them, and re-layouts  36 us (4%)
  other arithmetic  35.4 us (4%)
  starting transfers between devices  32.5 us (4%)
  between operations  14.8 us (2%)
    reduce_scatter x1, waiting for transfers between devices, body(): lax.psum_scatter(grad_wqkv, ('blk', 'ulysses'), scatter_dimension=0, tile...  125 us
    reduce_scatter x1, waiting for transfers between devices, body(): lax.psum_scatter(grad_win, ('blk', 'ulysses'), scatter_dimension=0, tiled...  91 us
    unnamed x2, blocking collectives  79.2 us
    ppermute x32, waiting for transfers between devices, from_behind(): lax.ppermute(value, axis, [(i, (i + by) % size) for i in range(size)])  76.3 us
    all_gather x1, waiting for transfers between devices, body(): lax.all_gather(in_weight, ('blk', 'ulysses'), axis=0, tiled=True)  59.9 us
    all_gather x1, waiting for transfers between devices, body(): lax.all_gather(out_weight, ('blk', 'ulysses'), axis=1, tiled=True)  54.5 us
    all_gather x1, waiting for transfers between devices, body(): key_piece = lax.all_gather(key_rows, 'blk', axis=1, tiled=True)  41.7 us
    all_gather x1, waiting for transfers between devices, body(): lax.all_gather(attn_out_weight, ('blk', 'ulysses'), axis=0, tiled=True)  36.1 us
  transfers between devices with their start and end apart: 46, of which 28 were waited for; matrix products, arithmetic and copies ran while one was open for 17% of the time, Pallas kernels for 0%

commit v1 on v0

--- a/solution.py
+++ b/solution.py
@@ -70,6 +70,18 @@
 def body(
     tokens, attn_gain, qkv_weight, attn_out_weight, mlp_gain, in_weight, out_weight, cotangent
 ):
+
+    def yards_store(field, a_name):
+        n_dev_all = lax.axis_size(a_name)
+        fields = [(ii, (ii + 1) % n_dev_all) for ii in range(n_dev_all)]
+        tile_out = [None] * n_dev_all
+        tile_out[n_dev_all - 1] = field
+        for hop_no in range(n_dev_all - 2, -1, -1):
+            tile_out[hop_no] = lax.ppermute(tile_out[hop_no + 1], a_name, fields)
+        fresh = jnp.concatenate(tile_out, axis=1)
+        block_next = (lax.axis_index(a_name) + 1) * field.shape[1]
+        return jnp.roll(fresh, shift=block_next, axis=1)
+
     sequences, per_device, model_width = tokens.shape
     groups = lax.axis_size("ulysses")
     cycle_size = lax.axis_size("blk")
@@ -105,7 +117,7 @@
     value_rows = headwise[:, :, 2]
     start_top = jnp.full((sequences, heads_here, group_rows), -1e30, jnp.float32)
     zeros_rows = jnp.zeros((sequences, group_rows, heads_here, HEAD), jnp.float32)
-    key_piece = lax.all_gather(key_rows, "blk", axis=1, tiled=True)
+    key_piece = yards_store(key_rows, "blk")
     value_piece = lax.all_gather(value_rows, "blk", axis=1, tiled=True)
     scores = (
         jnp.einsum("sqhd,skhd->shqk", queries, key_piece, preferred_element_type=jnp.float32)

time: 870 us -> 828 us (0.952)
  waiting for transfers between devices: 570 us -> 510 us
  blocking collectives: 79.2 us -> 93.3 us
  matrix products: 99.2 us -> 109 us
  local copies, waits for them, and re-layouts: 36 us -> 27 us
    ppermute x0 -> x7, waiting for transfers between devices: none -> 66 us  [yards_store(): tile_out[hop_no] = lax.ppermute(tile_out[hop_no + 1], a_name, fields)]
    all_gather x1 -> x0, waiting for transfers between devices: 41.7 us -> none  [body(): key_piece = lax.all_gather(key_rows, 'blk', axis=1, tiled=True)]
    all_gather x1, waiting for transfers between devices: 35.8 us -> 0.02 us  [body(): value_piece = lax.all_gather(value_rows, 'blk', axis=1, tiled=True)]
    all_gather x1, waiting for transfers between devices: 36.1 us -> 7.02 us  [body(): lax.all_gather(attn_out_weight, ('blk', 'ulysses'), axis=0, tiled=True)]
    all_to_all x0 -> x1, blocking collectives: none -> 14.2 us  [body(): lax.all_to_all(packed, 'ulysses', split_axis=3, concat_axis=1, tiled=True)]
    all_to_all x1 -> x0, waiting for transfers between devices: 10.7 us -> none  [body(): lax.all_to_all(packed, 'ulysses', split_axis=3, concat_axis=1, tiled=True)]
  transfers between devices with their start and end apart: 46 -> 51, of which waited for: 28 -> 32; matrix products, arithmetic and copies ran while one was open for 17% -> 18% of each run, Pallas kernels for 0% -> 0%
where the time goes in v1:
time: 828 us; the launch traced here: 826 us
  waiting for transfers between devices  510 us (62%)
  matrix products  109 us (13%)
  blocking collectives  93.3 us (11%)
  starting transfers between devices  36.6 us (4%)
  other arithmetic  36.2 us (4%)
  local copies, waits for them, and re-layouts  27 us (3%)
  between operations  14.6 us (2%)
    reduce_scatter x1, waiting for transfers between devices, body(): lax.psum_scatter(grad_wqkv, ('blk', 'ulysses'), scatter_dimension=0, tile...  125 us
    reduce_scatter x1, waiting for transfers between devices, body(): lax.psum_scatter(grad_win, ('blk', 'ulysses'), scatter_dimension=0, tiled...  87.9 us
    unnamed x2, blocking collectives  79.1 us
    ppermute x32, waiting for transfers between devices, from_behind(): lax.ppermute(value, axis, [(i, (i + by) % size) for i in range(size)])  69.1 us
    ppermute x7, waiting for transfers between devices, yards_store(): tile_out[hop_no] = lax.ppermute(tile_out[hop_no + 1], a_name, fields)  66 us
    all_gather x1, waiting for transfers between devices, body(): lax.all_gather(in_weight, ('blk', 'ulysses'), axis=0, tiled=True)  59.9 us
    all_gather x1, waiting for transfers between devices, body(): lax.all_gather(out_weight, ('blk', 'ulysses'), axis=1, tiled=True)  54.5 us
    ppermute x32, starting transfers between devices, from_behind(): lax.ppermute(value, axis, [(i, (i + by) % size) for i in range(size)])  21.3 us
  transfers between devices with their start and end apart: 51, of which 32 were waited for; matrix products, arithmetic and copies ran while one was open for 18% of the time, Pallas kernels for 0%

profile of v1, /device:TPU:0, one launch (start us, length us, event | category | flops | bytes accessed | tf_op | source)
XLA Modules:
  0.0 826.0 jit_solution(14625606097439817447)
XLA Ops:
  9.6 42.1 %all-reduce.8 = (bf16[768]{0:T(1024)(128)(2,1)S(1)}, bf16[768]{0:T(1024)(128)(2,1)S(1)}) all-reduce(bf16[768]{0:T(1024)(128)(2,1)S(1)} %dynamic-update-slice, bf16[768]{0:T(1024)(128)(2,1)S(1)} %dynamic-update-slice.1), channel_id=1, replica_groups=mesh['blk'=8,'ulysses'=4] {'blk','ulysses'}, use_global_device_ids=true, to_apply=%add.2 | all-reduce | flops 1536 | bytes 6144
  55.8 18.0 %all-gather.7.cloned.1.call-done = bf16[768,2304]{1,0:T(8,128)(2,1)} async-done(((bf16[24,2304]{1,0:T(8,128)(2,1)}), bf16[768,2304]{1,0:T(8,128)(2,1)}) %all-gather.7.cloned.1.call-update) | async-done | bytes 3538960 | tf_op jit(solution)/shard_map/all_gather | solution.py:93
  77.4 14.2 %all_to_all.60 = bf16[2,64,3,4,192]{4,1,2,0,3:T(8,128)(2,1)S(1)} all-to-all(bf16[2,64,3,4,192]{4,1,2,0,3:T(8,128)(2,1)S(1)} %copy.38), channel_id=1, replica_groups=mesh['blk'=8,'ulysses'=4] {'ulysses'}, dimensions={3} | all-to-all | bytes 1179648 | tf_op jit(solution)/shard_map/all_to_all | solution.py:108
  97.7 7.8 collective-permute-done.4
  105.5 10.1 %collective-permute-done.5 = bf16[2,256,3,64]{1,3,2,0:T(8,128)(2,1)S(1)} collective-permute-done((bf16[2,256,3,64]{1,3,2,0:T(8,128)(2,1)S(1)}, bf16[2,256,3,64]{1,3,2,0:T(8,128)(2,1)S(1)}, u32[]{:S(2)}, u32[]{:S(2)}) %collective-permute-start.5) | collective-permute-done | bytes 196640 | tf_op jit(solution)/shard_map/ppermute | solution.py:80
  115.7 8.4 %collective-permute-done.6 = bf16[2,256,3,64]{1,3,2,0:T(8,128)(2,1)S(1)} collective-permute-done((bf16[2,256,3,64]{1,3,2,0:T(8,128)(2,1)S(1)}, bf16[2,256,3,64]{1,3,2,0:T(8,128)(2,1)S(1)}, u32[]{:S(2)}, u32[]{:S(2)}) %collective-permute-start.6) | collective-permute-done | bytes 196640 | tf_op jit(solution)/shard_map/ppermute | solution.py:80
  124.1 11.0 %collective-permute-done.7 = bf16[2,256,3,64]{1,3,2,0:T(8,128)(2,1)S(1)} collective-permute-done((bf16[2,256,3,64]{1,3,2,0:T(8,128)(2,1)S(1)}, bf16[2,256,3,64]{1,3,2,0:T(8,128)(2,1)S(1)}, u32[]{:S(2)}, u32[]{:S(2)}) %collective-permute-start.7) | collective-permute-done | bytes 196640 | tf_op jit(solution)/shard_map/ppermute | solution.py:80
  135.2 11.5 %collective-permute-done.8 = bf16[2,256,3,64]{1,3,2,0:T(8,128)(2,1)S(1)} collective-permute-done((bf16[2,256,3,64]{1,3,2,0:T(8,128)(2,1)S(1)}, bf16[2,256,3,64]{1,3,2,0:T(8,128)(2,1)S(1)}, u32[]{:S(2)}, u32[]{:S(2)}) %collective-permute-start.8) | collective-permute-done | bytes 196640 | tf_op jit(solution)/shard_map/ppermute | solution.py:80
  146.8 8.6 %collective-permute-done.9 = bf16[2,256,3,64]{1,3,2,0:T(8,128)(2,1)S(1)} collective-permute-done((bf16[2,256,3,64]{1,3,2,0:T(8,128)(2,1)S(1)}, bf16[2,256,3,64]{1,3,2,0:T(8,128)(2,1)S(1)}, u32[]{:S(2)}, u32[]{:S(2)}) %collective-permute-start.9) | collective-permute-done | bytes 196640 | tf_op jit(solution)/shard_map/ppermute | solution.py:80
  155.4 8.5 %collective-permute-done.10 = bf16[2,256,3,64]{1,3,2,0:T(8,128)(2,1)S(1)} collective-permute-done((bf16[2,256,3,64]{1,3,2,0:T(8,128)(2,1)S(1)}, bf16[2,256,3,64]{1,3,2,0:T(8,128)(2,1)S(1)}, u32[]{:S(2)}, u32[]{:S(2)}) %collective-permute-start.10) | collective-permute-done | bytes 196640 | tf_op jit(solution)/shard_map/ppermute | solution.py:80
  173.3 8.2 fusion.59
  188.7 8.1 all-to-all-done.1
  206.3 59.9 %all-gather.11.cloned.1.call-done = bf16[768,2304]{1,0:T(8,128)(2,1)} async-done(((bf16[24,2304]{1,0:T(8,128)(2,1)}), bf16[768,2304]{1,0:T(8,128)(2,1)}) %all-gather.11.cloned.1.call-update) | async-done | bytes 3538960 | tf_op jit(solution)/shard_map/all_gather | solution.py:95
  268.8 54.5 %all-gather.13.cloned.1.call-done = bf16[1152,768]{0,1:T(8,128)(2,1)} async-done(((bf16[1152,24]{0,1:T(8,128)(2,1)}), bf16[1152,768]{0,1:T(8,128)(2,1)}) %all-gather.13.cloned.1.call-update) | async-done | bytes 1769488 | tf_op jit(solution)/shard_map/all_gather | solution.py:96
  350.1 183.2 %while.19 = (s32[]{:T(128)}, bf16[2,256,3,64]{1,3,2,0:T(8,128)(2,1)S(1)}, bf16[2,256,3,64]{1,3,2,0:T(8,128)(2,1)}, f32[2,256,3,64]{1,3,2,0:T(8,128)}, f32[2,256,...) while((s32[]{:T(128)}, ...), condition=%wide.region_10.11_spmd.clone, body=%wide.region_9.10_spmd.clone.sunk | while | flops 255787008 | bytes 15556913 | solution.py:211
  361.6 7.7 collective-permute-done.2
  384.6 12.8 %collective-permute-done.2 = bf16[2,256,3,64]{1,3,2,0:T(8,128)(2,1)} collective-permute-done((bf16[2,256,3,64]{1,3,2,0:T(8,128)(2,1)}, bf16[2,256,3,64]{1,3,2,0:T(8,128)(2,1)}, u32[]{:S(2)}, u32[]{:S(2)}) %collective-permute-start.2) | collective-permute-done | bytes 196640 | tf_op jit(solution)/shard_map/while/body/eval_jaxpr/ppermute | solution.py:13
  410.4 10.7 %collective-permute-done.2 = bf16[2,256,3,64]{1,3,2,0:T(8,128)(2,1)} collective-permute-done((bf16[2,256,3,64]{1,3,2,0:T(8,128)(2,1)}, bf16[2,256,3,64]{1,3,2,0:T(8,128)(2,1)}, u32[]{:S(2)}, u32[]{:S(2)}) %collective-permute-start.2) | collective-permute-done | bytes 196640 | tf_op jit(solution)/shard_map/while/body/eval_jaxpr/ppermute | solution.py:13
  433.4 9.1 %collective-permute-done.2 = bf16[2,256,3,64]{1,3,2,0:T(8,128)(2,1)} collective-permute-done((bf16[2,256,3,64]{1,3,2,0:T(8,128)(2,1)}, bf16[2,256,3,64]{1,3,2,0:T(8,128)(2,1)}, u32[]{:S(2)}, u32[]{:S(2)}) %collective-permute-start.2) | collective-permute-done | bytes 196640 | tf_op jit(solution)/shard_map/while/body/eval_jaxpr/ppermute | solution.py:13
  518.7 11.3 %collective-permute-done.2 = bf16[2,256,3,64]{1,3,2,0:T(8,128)(2,1)} collective-permute-done((bf16[2,256,3,64]{1,3,2,0:T(8,128)(2,1)}, bf16[2,256,3,64]{1,3,2,0:T(8,128)(2,1)}, u32[]{:S(2)}, u32[]{:S(2)}) %collective-permute-start.2) | collective-permute-done | bytes 196640 | tf_op jit(solution)/shard_map/while/body/eval_jaxpr/ppermute | solution.py:13
  544.0 11.3 %all-to-all-done.3 = bf16[2,256,3,1,192]{4,0,3,2,1:T(2,128)(2,1)S(1)} async-done(((bf16[2,256,3,1,192]{4,0,3,2,1:T(2,128)(2,1)}), bf16[2,256,3,1,192]{4,0,3,2,1:T(2,128)(2,1)S(1)}, u32[]{:S(2)}, u32[]{:S(2)}) %all-to-all-start.3) | async-done | bytes 589856 | tf_op jit(solution)/shard_map/all_to_all | solution.py:219
  568.0 37.0 %all-reduce.7 = (f32[768]{0:T(1024)S(1)}, f32[768]{0:T(1024)S(1)}) all-reduce(f32[768]{0:T(1024)S(1)} %get-tuple-element.116, f32[768]{0:T(1024)S(1)} %copy-done.20), channel_id=3, replica_groups=mesh['blk'=8,'ulysses'=4] {'blk','ulysses'}, use_global_device_ids=true, to_apply=%region_14.15.clone | all-reduce | flops 1536 | bytes 12288
  607.0 87.9 %reduce-scatter.11.cloned.1.call-done = f32[24,2304]{1,0:T(8,128)} async-done(((f32[768,2304]{1,0:T(8,128)}), f32[24,2304]{1,0:T(8,128)}) %reduce-scatter.11.cloned.1.call-update) | async-done | bytes 221200 | tf_op jit(solution)/shard_map/reduce_scatter | solution.py:231
  694.9 124.6 %reduce-scatter.7.cloned.1.call-done = f32[24,2304]{1,0:T(8,128)} async-done(((f32[768,2304]{1,0:T(8,128)}), f32[24,2304]{1,0:T(8,128)}) %reduce-scatter.7.cloned.1.call-update) | async-done | bytes 221200 | tf_op jit(solution)/shard_map/reduce_scatter | solution.py:229
  (315 shorter events, 227.8 us)
Async XLA Ops:
  7.2 66.7 %all-gather.7.cloned.1.call-start = ((), (), s32[]{:S(2)}) async-start(), calls=%async_computation.8 | async-start | bytes 3649536 | tf_op jit(solution)/shard_map/all_gather | solution.py:93
  7.9 165.4 %all-gather.15.cloned.1.call-start = ((), (), s32[]{:S(2)}) async-start(), calls=%async_computation.15 | async-start | bytes 1769472 | tf_op jit(solution)/shard_map/all_gather | solution.py:121
  93.9 110.5 %all-gather.9.cloned.1.call-start = ((), (), s32[]{:S(2)}) async-start(), calls=%async_computation.9 | async-start | bytes 1216512 | tf_op jit(solution)/shard_map/all_gather | solution.py:94
  94.6 171.5 %all-gather.11.cloned.1.call-start = ((), (), s32[]{:S(2)}) async-start(), calls=%async_computation.10 | async-start | bytes 3649536 | tf_op jit(solution)/shard_map/all_gather | solution.py:95
  95.2 228.1 %all-gather.13.cloned.1.call-start = ((), (), s32[]{:S(2)}) async-start(), calls=%async_computation.11 | async-start | bytes 1824768 | tf_op jit(solution)/shard_map/all_gather | solution.py:96
  188.7 418.3 %reduce-scatter.9.cloned.1.call-start = ((), (), s32[]{:S(2)}) async-start(), calls=%async_computation.13 | async-start | bytes 2433024 | tf_op jit(solution)/shard_map/reduce_scatter | solution.py:230
  331.0 276.0 %reduce-scatter.13.cloned.1.call-start = ((), (), s32[]{:S(2)}) async-start(), calls=%async_computation.16 | async-start | bytes 3649536
  341.9 352.9 %reduce-scatter.11.cloned.1.call-start = ((), (), s32[]{:S(2)}) async-start(), calls=%async_computation.14 | async-start | bytes 7299072 | tf_op jit(solution)/shard_map/reduce_scatter | solution.py:231
  350.2 22.7 %collective-permute-start = (bf16[2,256,3,64]{1,3,2,0:T(8,128)(2,1)S(1)}, bf16[2,256,3,64]{1,3,2,0:T(8,128)(2,1)S(1)}, u32[]{:S(2)}, u32[]{:S(2)}) collective-permute-start(bf16[2,256,3,64]{1,3,2,0:T(8,128)(2,1)S(1)} %copy.77), channel_id=1, source_target_pairs={{0,4},{4,8},{8,12},{12,16},{16,20},{20,24},{24,28},{28,0},{1,5},{5... | collective-permute-start | bytes 589832 | tf_op jit(solution)/shard_map/while/body/eval_jaxpr/ppermute | solution.py:13
  352.5 20.3 %collective-permute-start.1 = (bf16[2,256,3,64]{1,3,2,0:T(8,128)(2,1)S(1)}, bf16[2,256,3,64]{1,3,2,0:T(8,128)(2,1)}, u32[]{:S(2)}, u32[]{:S(2)}) collective-permute-start(bf16[2,256,3,64]{1,3,2,0:T(8,128)(2,1)S(1)} %copy.78), channel_id=1, source_target_pairs={{0,4},{4,8},{8,12},{12,16},{16,20},{20,24},{24,28},{28,0},{1,5},{5... | collective-permute-start | bytes 589832 | tf_op jit(solution)/shard_map/while/body/eval_jaxpr/ppermute | solution.py:13
  372.9 28.1 %collective-permute-start = (bf16[2,256,3,64]{1,3,2,0:T(8,128)(2,1)S(1)}, bf16[2,256,3,64]{1,3,2,0:T(8,128)(2,1)S(1)}, u32[]{:S(2)}, u32[]{:S(2)}) collective-permute-start(bf16[2,256,3,64]{1,3,2,0:T(8,128)(2,1)S(1)} %copy.77), channel_id=1, source_target_pairs={{0,4},{4,8},{8,12},{12,16},{16,20},{20,24},{24,28},{28,0},{1,5},{5... | collective-permute-start | bytes 589832 | tf_op jit(solution)/shard_map/while/body/eval_jaxpr/ppermute | solution.py:13
  373.9 27.1 %collective-permute-start.1 = (bf16[2,256,3,64]{1,3,2,0:T(8,128)(2,1)S(1)}, bf16[2,256,3,64]{1,3,2,0:T(8,128)(2,1)}, u32[]{:S(2)}, u32[]{:S(2)}) collective-permute-start(bf16[2,256,3,64]{1,3,2,0:T(8,128)(2,1)S(1)} %copy.78), channel_id=1, source_target_pairs={{0,4},{4,8},{8,12},{12,16},{16,20},{20,24},{24,28},{28,0},{1,5},{5... | collective-permute-start | bytes 589832 | tf_op jit(solution)/shard_map/while/body/eval_jaxpr/ppermute | solution.py:13
  377.9 19.5 %collective-permute-start.2 = (bf16[2,256,3,64]{1,3,2,0:T(8,128)(2,1)}, bf16[2,256,3,64]{1,3,2,0:T(8,128)(2,1)}, u32[]{:S(2)}, u32[]{:S(2)}) collective-permute-start(bf16[2,256,3,64]{1,3,2,0:T(8,128)(2,1)} %fusion.111), channel_id=1, source_target_pairs={{0,4},{4,8},{8,12},{12,16},{16,20},{20,24},{24,28},{28,0},{1,5},{5... | collective-permute-start | bytes 589832 | tf_op jit(solution)/shard_map/while/body/eval_jaxpr/ppermute | solution.py:13
  380.6 19.5 %collective-permute-start.3 = (bf16[2,256,3,64]{1,3,2,0:T(8,128)(2,1)}, bf16[2,256,3,64]{1,3,2,0:T(8,128)(2,1)S(1)}, u32[]{:S(2)}, u32[]{:S(2)}) collective-permute-start(bf16[2,256,3,64]{1,3,2,0:T(8,128)(2,1)} %fusion.112), channel_id=1, source_target_pairs={{0,4},{4,8},{8,12},{12,16},{16,20},{20,24},{24,28},{28,0},{1,5},{5... | collective-permute-start | bytes 589832 | tf_op jit(solution)/shard_map/while/body/eval_jaxpr/ppermute | solution.py:13
  401.0 23.1 %collective-permute-start = (bf16[2,256,3,64]{1,3,2,0:T(8,128)(2,1)S(1)}, bf16[2,256,3,64]{1,3,2,0:T(8,128)(2,1)S(1)}, u32[]{:S(2)}, u32[]{:S(2)}) collective-permute-start(bf16[2,256,3,64]{1,3,2,0:T(8,128)(2,1)S(1)} %copy.77), channel_id=1, source_target_pairs={{0,4},{4,8},{8,12},{12,16},{16,20},{20,24},{24,28},{28,0},{1,5},{5... | collective-permute-start | bytes 589832 | tf_op jit(solution)/shard_map/while/body/eval_jaxpr/ppermute | solution.py:13
  402.0 22.1 %collective-permute-start.1 = (bf16[2,256,3,64]{1,3,2,0:T(8,128)(2,1)S(1)}, bf16[2,256,3,64]{1,3,2,0:T(8,128)(2,1)}, u32[]{:S(2)}, u32[]{:S(2)}) collective-permute-start(bf16[2,256,3,64]{1,3,2,0:T(8,128)(2,1)S(1)} %copy.78), channel_id=1, source_target_pairs={{0,4},{4,8},{8,12},{12,16},{16,20},{20,24},{24,28},{28,0},{1,5},{5... | collective-permute-start | bytes 589832 | tf_op jit(solution)/shard_map/while/body/eval_jaxpr/ppermute | solution.py:13
  424.1 21.4 %collective-permute-start = (bf16[2,256,3,64]{1,3,2,0:T(8,128)(2,1)S(1)}, bf16[2,256,3,64]{1,3,2,0:T(8,128)(2,1)S(1)}, u32[]{:S(2)}, u32[]{:S(2)}) collective-permute-start(bf16[2,256,3,64]{1,3,2,0:T(8,128)(2,1)S(1)} %copy.77), channel_id=1, source_target_pairs={{0,4},{4,8},{8,12},{12,16},{16,20},{20,24},{24,28},{28,0},{1,5},{5... | collective-permute-start | bytes 589832 | tf_op jit(solution)/shard_map/while/body/eval_jaxpr/ppermute | solution.py:13
  425.1 20.4 %collective-permute-start.1 = (bf16[2,256,3,64]{1,3,2,0:T(8,128)(2,1)S(1)}, bf16[2,256,3,64]{1,3,2,0:T(8,128)(2,1)}, u32[]{:S(2)}, u32[]{:S(2)}) collective-permute-start(bf16[2,256,3,64]{1,3,2,0:T(8,128)(2,1)S(1)} %copy.78), channel_id=1, source_target_pairs={{0,4},{4,8},{8,12},{12,16},{16,20},{20,24},{24,28},{28,0},{1,5},{5... | collective-permute-start | bytes 589832 | tf_op jit(solution)/shard_map/while/body/eval_jaxpr/ppermute | solution.py:13
  445.5 19.8 %collective-permute-start = (bf16[2,256,3,64]{1,3,2,0:T(8,128)(2,1)S(1)}, bf16[2,256,3,64]{1,3,2,0:T(8,128)(2,1)S(1)}, u32[]{:S(2)}, u32[]{:S(2)}) collective-permute-start(bf16[2,256,3,64]{1,3,2,0:T(8,128)(2,1)S(1)} %copy.77), channel_id=1, source_target_pairs={{0,4},{4,8},{8,12},{12,16},{16,20},{20,24},{24,28},{28,0},{1,5},{5... | collective-permute-start | bytes 589832 | tf_op jit(solution)/shard_map/while/body/eval_jaxpr/ppermute | solution.py:13
  465.3 19.8 %collective-permute-start = (bf16[2,256,3,64]{1,3,2,0:T(8,128)(2,1)S(1)}, bf16[2,256,3,64]{1,3,2,0:T(8,128)(2,1)S(1)}, u32[]{:S(2)}, u32[]{:S(2)}) collective-permute-start(bf16[2,256,3,64]{1,3,2,0:T(8,128)(2,1)S(1)} %copy.77), channel_id=1, source_target_pairs={{0,4},{4,8},{8,12},{12,16},{16,20},{20,24},{24,28},{28,0},{1,5},{5... | collective-permute-start | bytes 589832 | tf_op jit(solution)/shard_map/while/body/eval_jaxpr/ppermute | solution.py:13
  485.1 19.9 %collective-permute-start = (bf16[2,256,3,64]{1,3,2,0:T(8,128)(2,1)S(1)}, bf16[2,256,3,64]{1,3,2,0:T(8,128)(2,1)S(1)}, u32[]{:S(2)}, u32[]{:S(2)}) collective-permute-start(bf16[2,256,3,64]{1,3,2,0:T(8,128)(2,1)S(1)} %copy.77), channel_id=1, source_target_pairs={{0,4},{4,8},{8,12},{12,16},{16,20},{20,24},{24,28},{28,0},{1,5},{5... | collective-permute-start | bytes 589832 | tf_op jit(solution)/shard_map/while/body/eval_jaxpr/ppermute | solution.py:13
  505.0 28.4 %collective-permute-start = (bf16[2,256,3,64]{1,3,2,0:T(8,128)(2,1)S(1)}, bf16[2,256,3,64]{1,3,2,0:T(8,128)(2,1)S(1)}, u32[]{:S(2)}, u32[]{:S(2)}) collective-permute-start(bf16[2,256,3,64]{1,3,2,0:T(8,128)(2,1)S(1)} %copy.77), channel_id=1, source_target_pairs={{0,4},{4,8},{8,12},{12,16},{16,20},{20,24},{24,28},{28,0},{1,5},{5... | collective-permute-start | bytes 589832 | tf_op jit(solution)/shard_map/while/body/eval_jaxpr/ppermute | solution.py:13
  506.0 27.4 %collective-permute-start.1 = (bf16[2,256,3,64]{1,3,2,0:T(8,128)(2,1)S(1)}, bf16[2,256,3,64]{1,3,2,0:T(8,128)(2,1)}, u32[]{:S(2)}, u32[]{:S(2)}) collective-permute-start(bf16[2,256,3,64]{1,3,2,0:T(8,128)(2,1)S(1)} %copy.78), channel_id=1, source_target_pairs={{0,4},{4,8},{8,12},{12,16},{16,20},{20,24},{24,28},{28,0},{1,5},{5... | collective-permute-start | bytes 589832 | tf_op jit(solution)/shard_map/while/body/eval_jaxpr/ppermute | solution.py:13
  543.6 275.9 %reduce-scatter.7.cloned.1.call-start = ((), (), s32[]{:S(2)}) async-start(), calls=%async_computation.12 | async-start | bytes 7299072 | tf_op jit(solution)/shard_map/reduce_scatter | solution.py:229
  (57 other events, 897.8 us)
Sparse Core Ops, SparseCore 0:
  10.9 62.8 all-gather.6
  94.0 50.6 all-gather.14
  147.7 56.6 all-gather.8
  207.1 58.9 all-gather.10
  268.8 54.4 all-gather.12
  331.1 112.0 reduce-scatter.8
  450.1 119.5 reduce-scatter.12
  576.9 117.9 reduce-scatter.10
  701.1 118.2 reduce-scatter.6
